TPU v7x, 512 devices: a whole 4x8x8 slice. The times are simulated.
512 devices in a mesh: samp: 8 (over z), pair: 16 (over y_lo, x), recv: 4 (over y_hi, core).
Axes of the slice: x: 4, y: 8 (y_hi: 2, y_lo: 4; y = y_hi * 4 + y_lo), z: 8, core: 2. Of those that a mesh axis runs over, the one named last changes fastest.
Arguments:
- cell_expression: bfloat16 [32, 16384, 2048], P('samp', 'recv', 'pair'), may hold values from 0 to 24
- cell_labels: int32 [32, 16384], P('samp', 'recv'), may hold values from 0 to 127, as said below
- ligand_gene: int32 [2048], P('pair'), may hold values from 0 to 2047
- receptor_gene: int32 [2048], P('pair'), may hold values from 0 to 2047
- pair_factor: bfloat16 [2048, 32], P('pair'), may hold values from -0.53033009 to 0.53033009
- sender_factor: bfloat16 [128, 32], replicated, may hold values from -0.5 to 0.5
- receiver_factor: bfloat16 [128, 32], P('recv'), may hold values from -2.5 to 2.5
Outputs:
- sample_factor: float32 [32, 32], P('samp')
Inputs may be any that keep to these rules, and one draw needn't show every extreme that they name: `cell_labels`: in every sample one cell type has no cell.
All inputs are finite; a program needn't handle non-finite values.
Results may differ from a plain program's by a relative error of at most 0.0051.
Values may be sent and summed in bfloat16 or wider, within the bound.
No kernel may reach another device: no remote copies, remote signals or barrier semaphores. Data moves between devices by JAX's collectives and lax.ppermute only.
A program may use at most 64 MiB of HBM per device.

v0:
```python
import jax
import jax.numpy as jnp
from jax import lax
from jax.sharding import PartitionSpec as P


def body(
    cell_expression,
    cell_labels,
    ligand_gene,
    receptor_gene,
    pair_factor,
    sender_factor,
    receiver_factor,
):
    clusters = sender_factor.shape[0]
    factor_rank = sender_factor.shape[1]
    block_width = receiver_factor.shape[0]
    member = (
        cell_labels[:, :, None] == jnp.arange(clusters, dtype=jnp.int32)[None, None, :]
    ).astype(jnp.bfloat16)
    part_sums = jnp.einsum(
        "scg,sck->sgk", cell_expression, member, preferred_element_type=jnp.float32
    )
    part_counts = jnp.sum(member, axis=1, dtype=jnp.float32)
    receiver_start = lax.axis_index("recv") * block_width
    cluster_total, cell_count = lax.psum((part_sums, part_counts), "recv")
    cluster_mean = (cluster_total / jnp.maximum(cell_count, 1.0)[:, None, :]).astype(jnp.bfloat16)
    segment = lax.all_gather(cluster_mean, "pair", axis=1, tiled=True)
    ligand_table = jnp.einsum(
        "sga,ar->srg", segment, sender_factor, preferred_element_type=jnp.float32
    ).astype(jnp.bfloat16)
    receiver_columns = lax.dynamic_slice_in_dim(segment, receiver_start, block_width, 2)
    receptor_table = jnp.einsum(
        "sgb,br->srg", receiver_columns, receiver_factor, preferred_element_type=jnp.float32
    ).astype(jnp.bfloat16)
    joined_tables = jnp.concatenate([ligand_table, receptor_table], axis=1)
    ligand_rows = jnp.take(joined_tables[:, :factor_rank, :], ligand_gene, axis=2).astype(
        jnp.float32
    )
    receptor_rows = jnp.take(joined_tables[:, factor_rank:, :], receptor_gene, axis=2).astype(
        jnp.float32
    )
    pair_weights = pair_factor.astype(jnp.float32).T
    partial_product = jnp.sum(ligand_rows * receptor_rows * pair_weights[None, :, :], axis=2)
    pair_gram = jnp.einsum(
        "pr,pq->rq", pair_factor, pair_factor, preferred_element_type=jnp.float32
    )
    sender_gram = jnp.einsum(
        "pr,pq->rq", sender_factor, sender_factor, preferred_element_type=jnp.float32
    )
    receiver_gram = jnp.einsum(
        "pr,pq->rq", receiver_factor, receiver_factor, preferred_element_type=jnp.float32
    )
    product_total = lax.psum(partial_product, ("pair", "recv"))
    pair_gram = lax.psum(pair_gram, "pair")
    receiver_gram = lax.psum(receiver_gram, "recv")
    hadamard = pair_gram * sender_gram * receiver_gram
    cholesky_factor = jnp.linalg.cholesky(hadamard)
    solution = jax.scipy.linalg.cho_solve((cholesky_factor, True), product_total.T)
    return solution.T


def solution(mesh):
    placed = (
        P("samp", "recv", "pair"),
        P("samp", "recv"),
        P("pair"),
        P("pair"),
        P("pair", None),
        P(),
        P("recv", None),
    )
    return jax.shard_map(
        body, mesh=mesh, in_specs=placed, out_specs=P("samp", None), check_vma=False
    )
```

profile of v0, /device:TPU:9, one launch (start us, length us, event | category | flops | bytes accessed | tf_op | source)
XLA Modules:
  0.0 325.3 jit_solution(4889094992332328623)
XLA Ops:
  6.6 4.6 %fusion.3 = f32[4,128,128]{1,2,0:T(8,128)} fusion(bf16[4,4096,128]{2,1,0:T(8,128)(2,1)} %param.9, s32[4,4096]{1,0:T(4,128)} %param.10), kind=kOutput, calls=%fused_computation.9 | convolution fusion | flops 538968064 | bytes 4521984 | tf_op jit(solution)/shard_map/scg,sck->sgk/dot_general | solution.py:22
  11.3 0.2 fusion.16
  11.5 1.3 convert_reduce_fusion
  12.8 18.3 %all-reduce = (f32[4,128]{1,0:T(4,128)S(1)}, f32[32,32]{0,1:T(8,128)S(1)}) all-reduce(f32[4,128]{1,0:T(4,128)S(1)} %convert_reduce_fusion, f32[32,32]{0,1:T(8,128)S(1)} %fusion.16), channel_id=1, replica_groups=mesh['samp'=8,'pair'=16,'recv'=4] {'recv'}, use_global_device_ids=true, to_apply=%region_6.7 | all-reduce | flops 1536 | bytes 12288 | tf_op jit(solution)/shard_map/psum | solution.py:27
  31.0 43.7 %all-reduce.3.cloned.1.call-done = f32[4,128,128]{1,2,0:T(8,128)} async-done(((f32[4,128,128]{1,2,0:T(8,128)}), f32[4,128,128]{1,2,0:T(8,128)}) %all-reduce.3.cloned.1.call-update) | async-done | bytes 262160 | tf_op jit(solution)/shard_map/psum | solution.py:27
  74.7 1.7 divide_convert_fusion
  76.5 0.1 fusion.15
  76.6 57.9 %psum.35 = f32[32,32]{0,1:T(8,128)S(1)} all-reduce(f32[32,32]{0,1:T(8,128)S(1)} %fusion.15), channel_id=1, replica_groups=mesh['samp'=8,'pair'=16,'recv'=4] {'pair'}, use_global_device_ids=true, to_apply=%region_0.0 | all-reduce | flops 1024 | bytes 8192 | tf_op jit(solution)/shard_map/psum | solution.py:56
  134.5 0.1 fusion.4
  134.7 2.9 cholesky.16
  137.6 0.6 compare_reduce_fusion
  138.3 0.7 fusion.6
  138.9 2.5 custom-call.10
  141.6 0.3 all-gather.2.cloned.1.call-done
  141.8 2.0 convolution_convert_fusion
  143.8 1.4 copy.23
  145.2 1.4 convolution_convert_fusion.1
  146.6 2.5 copy.24
  149.1 0.7 gather_fusion
  149.9 2.3 gather_fusion.1
  152.2 0.3 multiply_reduce_fusion
  152.6 164.9 %psum.39 = f32[4,32]{1,0:T(4,128)S(1)} all-reduce(f32[4,32]{1,0:T(4,128)S(1)} %multiply_reduce_fusion), channel_id=1, replica_groups=mesh['samp'=8,'pair'=16,'recv'=4] {'pair','recv'}, use_global_device_ids=true, to_apply=%region_8.10 | all-reduce | flops 128 | bytes 1024 | tf_op jit(solution)/shard_map/psum | solution.py:55
  317.5 0.2 fusion.9
  317.7 0.8 fusion.7
  (27 shorter events, 0.4 us)
Async XLA Ops:
  6.5 127.9 %copy-start = (bf16[128,32]{0,1:T(8,128)(2,1)S(1)}, bf16[128,32]{0,1:T(8,128)(2,1)}, u32[]{:S(2)}) copy-start(bf16[128,32]{0,1:T(8,128)(2,1)} %param.14) | copy-start | bytes 24580
  6.5 4.9 %copy-start.2 = (s32[4,4096]{1,0:T(4,128)S(1)}, s32[4,4096]{1,0:T(4,128)}, u32[]{:S(2)}) copy-start(s32[4,4096]{1,0:T(4,128)} %param.10) | copy-start | bytes 196612
  6.5 4.7 %copy-start.3 = (bf16[32,32]{1,0:T(8,128)(2,1)S(1)}, bf16[32,32]{1,0:T(8,128)(2,1)}, u32[]{:S(2)}) copy-start(bf16[32,32]{1,0:T(8,128)(2,1)} %param.15) | copy-start | bytes 6148
  6.5 69.9 %copy-start.1 = (bf16[128,32]{0,1:T(8,128)(2,1)S(1)}, bf16[128,32]{0,1:T(8,128)(2,1)}, u32[]{:S(2)}) copy-start(bf16[128,32]{0,1:T(8,128)(2,1)} %param.13) | copy-start | bytes 24580
  6.5 134.9 %copy-start.4 = (s32[128]{0:T(128)S(1)}, s32[128]{0:T(128)}, u32[]{:S(2)}) copy-start(s32[128]{0:T(128)} %param.12) | copy-start | bytes 1540
  6.5 135.0 %copy-start.5 = (s32[128]{0:T(128)S(1)}, s32[128]{0:T(128)}, u32[]{:S(2)}) copy-start(s32[128]{0:T(128)} %param.11) | copy-start | bytes 1540
  6.6 68.1 %all-reduce.3.cloned.1.call-start = ((), (), s32[]{:S(2)}) async-start(), calls=%async_computation | async-start | bytes 524288 | tf_op jit(solution)/shard_map/psum | solution.py:27
  11.2 130.6 %all-gather.2.cloned.1.call-start = ((), (), s32[]{:S(2)}) async-start(), calls=%async_computation.1 | async-start | bytes 2228224 | tf_op jit(solution)/shard_map/all_gather | solution.py:29
Sparse Core Ops, SparseCore 0:
  11.3 63.2 all-reduce.2
  76.9 64.9 all-gather.1
where the time goes:
time: 326 us; the launch traced here: 325 us
  blocking collectives  241 us (74%)
  waiting for transfers between devices  43.9 us (13%)
  between operations  13.6 us (4%)
  other arithmetic  10.1 us (3%)
  matrix products  9.4 us (3%)
  local copies, waits for them, and re-layouts  7.17 us (2%)
    psum x1, blocking collectives, body(): product_total = lax.psum(partial_product, ('pair', 'recv'))  165 us
    psum x1, blocking collectives, body(): pair_gram = lax.psum(pair_gram, 'pair')  57.9 us
    psum x1, waiting for transfers between devices, body(): cluster_total, cell_count = lax.psum((part_sums, part_counts), 'recv')  43.7 us
    psum x1, blocking collectives, body(): cluster_total, cell_count = lax.psum((part_sums, part_counts), 'recv')  18.3 us
  transfers between devices with their start and end apart: 2, of which 2 were waited for; matrix products, arithmetic and copies ran while one was open for 3% of the time, Pallas kernels for 0%

commit v1 on v0

--- a/solution.py
+++ b/solution.py
@@ -1,7 +1,18 @@
+import functools
 import jax
 import jax.numpy as jnp
 from jax import lax
 from jax.sharding import PartitionSpec as P
+from jax.lax import psum
+
+
+def name_grid(original, a_name, named_axis):
+    for k in (a_name, named_axis):
+        original = psum(original, k)
+    return original
+
+
+match_marks = functools.partial(name_grid, a_name="pair", named_axis="recv")
 
 
 def body(
@@ -52,7 +63,7 @@
     receiver_gram = jnp.einsum(
         "pr,pq->rq", receiver_factor, receiver_factor, preferred_element_type=jnp.float32
     )
-    product_total = lax.psum(partial_product, ("pair", "recv"))
+    product_total = match_marks(partial_product)
     pair_gram = lax.psum(pair_gram, "pair")
     receiver_gram = lax.psum(receiver_gram, "recv")
     hadamard = pair_gram * sender_gram * receiver_gram

time: 326 us -> 274 us (0.84)
  the two profiles are of different devices: /device:TPU:9 before, /device:TPU:1 now
where the time goes in v1:
time: 274 us
  blocking collectives  122 us (45%)
  waiting for transfers between devices  112 us (41%)
  between operations  13.6 us (5%)
  other arithmetic  10.1 us (4%)
  matrix products  9.45 us (3%)
  local copies, waits for them, and re-layouts  7.16 us (3%)
    psum x2, blocking collectives, name_grid(): original = psum(original, k)  106 us
    all_gather x1, waiting for transfers between devices, body(): segment = lax.all_gather(cluster_mean, 'pair', axis=1, tiled=True)  63.7 us
    psum x1, waiting for transfers between devices, body(): cluster_total, cell_count = lax.psum((part_sums, part_counts), 'recv')  48.2 us
    psum x1, blocking collectives, body(): cluster_total, cell_count = lax.psum((part_sums, part_counts), 'recv')  15.8 us
  transfers between devices with their start and end apart: 2, of which 2 were waited for; matrix products, arithmetic and copies ran while one was open for 1% of the time, Pallas kernels for 0%

profile of v1, /device:TPU:1, one launch (start us, length us, event | category | flops | bytes accessed | tf_op | source)
XLA Modules:
  0.0 274.2 jit_solution(15361561997868056688)
XLA Ops:
  6.6 4.6 %fusion.3 = f32[4,128,128]{1,2,0:T(8,128)} fusion(bf16[4,4096,128]{2,1,0:T(8,128)(2,1)} %param.9, s32[4,4096]{1,0:T(4,128)} %param.10), kind=kOutput, calls=%fused_computation.9 | convolution fusion | flops 538968064 | bytes 4521984 | tf_op jit(solution)/shard_map/scg,sck->sgk/dot_general | solution.py:33
  11.3 1.3 convert_reduce_fusion
  12.6 15.8 %psum.45 = f32[4,128]{1,0:T(4,128)S(1)} all-reduce(f32[4,128]{1,0:T(4,128)S(1)} %convert_reduce_fusion), channel_id=1, replica_groups=mesh['samp'=8,'pair'=16,'recv'=4] {'recv'}, use_global_device_ids=true, to_apply=%region_6.7 | all-reduce | flops 512 | bytes 4096 | tf_op jit(solution)/shard_map/psum | solution.py:38
  28.4 48.2 %all-reduce.4.cloned.1.call-done = f32[4,128,128]{1,2,0:T(8,128)} async-done(((f32[4,128,128]{1,2,0:T(8,128)}), f32[4,128,128]{1,2,0:T(8,128)}) %all-reduce.4.cloned.1.call-update) | async-done | bytes 262160 | tf_op jit(solution)/shard_map/psum | solution.py:38
  76.6 1.7 divide_convert_fusion
  78.5 0.1 fusion.15
  78.7 0.2 fusion.16
  78.9 63.7 %all-gather.2.cloned.1.call-done = bf16[4,2048,128]{1,2,0:T(8,128)(2,1)} async-done(((bf16[4,128,128]{1,2,0:T(8,128)(2,1)}), bf16[4,2048,128]{1,2,0:T(8,128)(2,1)}) %all-gather.2.cloned.1.call-update) | async-done | bytes 2097168 | tf_op jit(solution)/shard_map/all_gather | solution.py:40
  142.6 2.0 convolution_convert_fusion
  144.6 1.4 copy.23
  146.0 1.4 convolution_convert_fusion.1
  147.4 2.5 copy.24
  149.9 0.7 gather_fusion
  150.6 2.3 gather_fusion.1
  153.0 0.3 multiply_reduce_fusion
  153.3 64.3 %all-reduce = (f32[4,32]{1,0:T(4,128)S(1)}, f32[32,32]{0,1:T(8,128)S(1)}) all-reduce(f32[4,32]{1,0:T(4,128)S(1)} %multiply_reduce_fusion, f32[32,32]{0,1:T(8,128)S(1)} %fusion.15), channel_id=1, replica_groups=mesh['samp'=8,'pair'=16,'recv'=4] {'pair'}, use_global_device_ids=true, to_apply=%region_8.10 | all-reduce | flops 1152 | bytes 9216 | tf_op jit(solution)/shard_map/psum | solution.py:11
  217.6 41.8 %all-reduce.1 = (f32[4,32]{1,0:T(4,128)S(1)}, f32[32,32]{0,1:T(8,128)S(1)}) all-reduce(f32[4,32]{1,0:T(4,128)S(1)} %get-tuple-element.6, f32[32,32]{0,1:T(8,128)S(1)} %fusion.16), channel_id=1, replica_groups=mesh['samp'=8,'pair'=16,'recv'=4] {'recv'}, use_global_device_ids=true, to_apply=%region_9.11 | all-reduce | flops 1152 | bytes 9216 | tf_op jit(solution)/shard_map/psum | solution.py:11
  259.4 0.1 fusion.4
  259.6 2.9 %cholesky.16 = f32[32,32]{1,0:T(8,128)S(1)} custom-call(f32[32,32]{1,0:T(8,128)S(1)} %fusion.11), custom_call_target="Cholesky" | custom-call | tf_op jit(solution)/shard_map/jit(cholesky)/cholesky | solution.py:70
  262.6 0.6 compare_reduce_fusion
  263.2 0.7 fusion.6
  263.9 2.4 custom-call.10
  266.3 0.2 fusion.9
  266.6 0.8 fusion.7
  (27 shorter events, 0.4 us)
Async XLA Ops:
  6.5 72.1 %copy-start = (bf16[32,32]{1,0:T(8,128)(2,1)S(1)}, bf16[32,32]{1,0:T(8,128)(2,1)}, u32[]{:S(2)}) copy-start(bf16[32,32]{1,0:T(8,128)(2,1)} %param.15) | copy-start | bytes 6148
  6.5 4.8 %copy-start.3 = (s32[4,4096]{1,0:T(4,128)S(1)}, s32[4,4096]{1,0:T(4,128)}, u32[]{:S(2)}) copy-start(s32[4,4096]{1,0:T(4,128)} %param.10) | copy-start | bytes 196612
  6.5 71.8 %copy-start.2 = (bf16[128,32]{0,1:T(8,128)(2,1)S(1)}, bf16[128,32]{0,1:T(8,128)(2,1)}, u32[]{:S(2)}) copy-start(bf16[128,32]{0,1:T(8,128)(2,1)} %param.13) | copy-start | bytes 24580
  6.5 71.9 %copy-start.4 = (s32[128]{0:T(128)S(1)}, s32[128]{0:T(128)}, u32[]{:S(2)}) copy-start(s32[128]{0:T(128)} %param.12) | copy-start | bytes 1540
  6.5 71.9 %copy-start.5 = (s32[128]{0:T(128)S(1)}, s32[128]{0:T(128)}, u32[]{:S(2)}) copy-start(s32[128]{0:T(128)} %param.11) | copy-start | bytes 1540
  6.5 136.0 %copy-start.1 = (bf16[128,32]{0,1:T(8,128)(2,1)S(1)}, bf16[128,32]{0,1:T(8,128)(2,1)}, u32[]{:S(2)}) copy-start(bf16[128,32]{0,1:T(8,128)(2,1)} %param.14) | copy-start | bytes 24580
  6.6 70.0 %all-reduce.4.cloned.1.call-start = ((), (), s32[]{:S(2)}) async-start(), calls=%async_computation | async-start | bytes 524288 | tf_op jit(solution)/shard_map/psum | solution.py:38
  11.2 131.3 %all-gather.2.cloned.1.call-start = ((), (), s32[]{:S(2)}) async-start(), calls=%async_computation.1 | async-start | bytes 2228224 | tf_op jit(solution)/shard_map/all_gather | solution.py:40
Sparse Core Ops, SparseCore 0:
  11.4 65.1 all-reduce.3
  78.8 63.7 all-gather.1
